TPU v7x, 32 devices: a whole 2x2x4 slice. The times are simulated.
32 devices in a mesh: seq: 8 (over y, x, core), tp: 4 (over z).
Axes of the slice: x: 2, y: 2, z: 4, core: 2. Of those that a mesh axis runs over, the one named last changes fastest.
Arguments:
- byte_states: bfloat16 [2048, 1024], P('seq'), may hold values from -6 to 6
- enc_gain: bfloat16 [1024], replicated, may hold values from 0.25 to 1.75
- enc_qkv: bfloat16 [3, 1024, 1024], P(None, None, 'tp')
- enc_proj_out: bfloat16 [1024, 1024], P('tp'), may hold values from -0.1875 to 0.1875
- starts: int32 [8, 64], P('seq'), may hold values from 0 to 2048, as said below
- counts: int32 [8], P('seq'), may hold values from 32 to 64, as said below
- lift: bfloat16 [1024, 4096], P(None, 'tp')
- cross_kv: bfloat16 [2, 1024, 4096], P(None, None, 'tp')
- latent_gain: bfloat16 [4096], replicated, may hold values from 0.25 to 1.75
- lat_qkv: bfloat16 [3, 4096, 2048], P(None, 'seq', 'tp')
- lat_proj_out: bfloat16 [2048, 4096], P('tp', 'seq'), may hold values from -0.75 to 0.75
Outputs:
- byte_out: bfloat16 [2048, 1024], P('seq')
- latent_out: bfloat16 [512, 4096], P('seq', 'tp')
Inputs may be any that keep to these rules, and one draw needn't show every extreme that they name: `starts`: row s lists in increasing order the first byte (counted over all 2048 bytes) of each patch beginning in bytes s * 256 to (s + 1) * 256 - 1, then 2048 in unused places. Byte 0 begins a patch; every row's first patch begins fewer than 8 bytes into its block, and in some row exactly 7 bytes in. counts[s] is the number of patches listed in row s of starts; some row holds 64.
All inputs are finite; a program needn't handle non-finite values.
Results may differ from a plain program's by a relative error of at most 0.018.
Values may be sent and summed in bfloat16 or wider, within the bound.
A program may use at most 128 MiB of HBM per device.

v0:
```python
import math
import jax
import jax.numpy as jnp
from jax import lax
from jax.sharding import PartitionSpec as P

EH = 64
HD = 128
WIN = 512
SPILL = 8
epsilon = 1e-05
rope_base = 500000.0
far_position = 1 << 30


def from_behind(value, axis, steps):
    count = lax.axis_size(axis)
    leading, last = (max(0, -steps), min(count, count - steps))
    return lax.ppermute(value, axis, [(source, source + steps) for source in range(leading, last)])


def prefix(value, axis, join, neutral):
    count, mine = (lax.axis_size(axis), lax.axis_index(axis))
    pieces = lax.all_gather(value, axis)
    subtotal = jnp.full_like(value, 0) + jnp.asarray(neutral, value.dtype)

    def hop(position, subtotal):
        longer = join(subtotal, pieces[position])
        return jnp.where(position < mine, longer, subtotal)

    return lax.fori_loop(0, count - 1, hop, subtotal)


def shortened(value):

    def short(part):
        return part.astype(jnp.bfloat16) if part.dtype == jnp.float32 else part

    return jax.tree.map(short, value)


def rms_scale(values, gain_row):
    mean_square = jnp.mean(values * values, axis=-1, keepdims=True)
    return values * lax.rsqrt(mean_square + epsilon) * gain_row


def masked_softmax(scores, allowed):
    scores = jnp.where(allowed, scores, -1e30)
    largest = jnp.max(scores, axis=-1, keepdims=True)
    raised = jnp.where(allowed, jnp.exp(scores - largest), 0.0)
    return raised / jnp.sum(raised, axis=-1, keepdims=True)


def rotate(values, position):
    halfway = values.shape[-1] // 2
    frequency = jnp.power(
        rope_base, -2.0 * jnp.arange(halfway, dtype=jnp.float32) / values.shape[-1]
    )
    angles = position.astype(jnp.float32)[:, None] * frequency[None, :]
    cosine = jnp.cos(angles)[:, None, :]
    sine_rows = jnp.sin(angles)[:, None, :]
    lower_half = values[..., :halfway]
    upper_half = values[..., halfway:]
    return jnp.concatenate(
        [
            lower_half * cosine - upper_half * sine_rows,
            upper_half * cosine + lower_half * sine_rows,
        ],
        axis=-1,
    )


def patch_block(extended, first_byte, end_byte, in_use, anchor, lift, cross_kv):
    columns = anchor + jnp.arange(extended.shape[0], dtype=jnp.int32)
    inside = (
        (columns[None, :] >= first_byte[:, None])
        & (columns[None, :] < end_byte[:, None])
        & in_use[:, None]
    )
    member = inside.astype(jnp.bfloat16)
    totals = jnp.dot(member, extended, preferred_element_type=jnp.float32)
    lengths = jnp.maximum(jnp.sum(inside.astype(jnp.float32), axis=1), 1.0)
    pooled = (totals / lengths[:, None]).astype(jnp.bfloat16)
    lifted = jnp.dot(pooled, lift, preferred_element_type=jnp.float32)
    key_rows = jnp.dot(extended, cross_kv[0], preferred_element_type=jnp.float32).astype(
        jnp.bfloat16
    )
    value_rows = jnp.dot(extended, cross_kv[1], preferred_element_type=jnp.float32).astype(
        jnp.bfloat16
    )
    slot_total = first_byte.shape[0]
    head_count = lifted.shape[1] // HD
    queries = lifted.astype(jnp.bfloat16).reshape(slot_total, head_count, HD)
    scores = jnp.einsum(
        "phd,khd->hpk",
        queries,
        key_rows.reshape(-1, head_count, HD),
        preferred_element_type=jnp.float32,
    ) * (1.0 / math.sqrt(HD))
    allowed = inside | (~in_use)[:, None] & (columns[None, :] == anchor)
    weights = masked_softmax(scores, allowed[None]).astype(jnp.bfloat16)
    crossed = jnp.einsum(
        "hpk,khd->phd",
        weights,
        value_rows.reshape(-1, head_count, HD),
        preferred_element_type=jnp.float32,
    )
    crossed = crossed.reshape(slot_total, head_count * HD)
    return jnp.where(in_use[:, None], lifted + crossed, 0.0).astype(jnp.bfloat16)


def add_counts(earlier, later):
    return earlier + later


def shards(
    byte_states,
    enc_gain,
    enc_qkv,
    enc_proj_out,
    starts,
    counts,
    lift,
    cross_kv,
    latent_gain,
    lat_qkv,
    lat_proj_out,
):
    byte_rows = byte_states.shape[0]
    anchor = lax.axis_index("seq") * byte_rows
    states = byte_states.astype(jnp.float32)
    normed = rms_scale(states, enc_gain.astype(jnp.float32)).astype(jnp.bfloat16)
    projected = jnp.einsum(
        "bd,idc->ibc", normed, enc_qkv, preferred_element_type=jnp.float32
    ).astype(jnp.bfloat16)
    reach_blocks = max(WIN // byte_rows, 1)
    tail_rows = min(WIN, byte_rows)
    key_parts = []
    value_parts = []
    for distance in range(reach_blocks, 0, -1):
        moved_keys, moved_values = from_behind(
            (projected[1, byte_rows - tail_rows :], projected[2, byte_rows - tail_rows :]),
            "seq",
            distance,
        )
        key_parts.append(moved_keys)
        value_parts.append(moved_values)
    key_rows = jnp.concatenate(key_parts + [projected[1]], axis=0)
    value_rows = jnp.concatenate(value_parts + [projected[2]], axis=0)
    head_count = projected.shape[2] // EH
    scores = jnp.einsum(
        "qhd,khd->hqk",
        projected[0].reshape(byte_rows, head_count, EH),
        key_rows.reshape(-1, head_count, EH),
        preferred_element_type=jnp.float32,
    ) * (1.0 / math.sqrt(EH))
    query_pos = anchor + jnp.arange(byte_rows, dtype=jnp.int32)
    key_pos = anchor - WIN + jnp.arange(WIN + byte_rows, dtype=jnp.int32)
    allowed = (
        (key_pos[None, :] <= query_pos[:, None])
        & (key_pos[None, :] > query_pos[:, None] - WIN)
        & (key_pos[None, :] >= 0)
    )
    weights = masked_softmax(scores, allowed[None]).astype(jnp.bfloat16)
    attended = jnp.einsum(
        "hqk,khd->qhd",
        weights,
        value_rows.reshape(-1, head_count, EH),
        preferred_element_type=jnp.float32,
    )
    attended = attended.reshape(byte_rows, head_count * EH).astype(jnp.bfloat16)
    blended = lax.psum(jnp.dot(attended, enc_proj_out, preferred_element_type=jnp.float32), "tp")
    encoded = (states + blended).astype(jnp.bfloat16)
    patch_count = counts[0]
    local_starts = starts[0]
    first_local = (local_starts[0:1] - anchor).astype(jnp.bfloat16)
    next_rows, next_first = from_behind((encoded[:SPILL], first_local), "seq", -1)
    next_first = next_first.astype(jnp.int32)[0]
    extended = jnp.concatenate([encoded, next_rows], axis=0)
    slot_ids = jnp.arange(local_starts.shape[0], dtype=jnp.int32)
    in_use = slot_ids < patch_count
    following = jnp.concatenate([local_starts[1:], jnp.zeros((1,), jnp.int32)])
    patch_end = jnp.where(slot_ids + 1 < patch_count, following, anchor + byte_rows + next_first)
    patches = patch_block(extended, local_starts, patch_end, in_use, anchor, lift, cross_kv)
    offset = prefix(counts, "seq", add_counts, jnp.zeros((1,), jnp.int32))[0]
    position = offset + slot_ids
    slot_total = patches.shape[0]
    full_rows = lax.all_gather(patches, "tp", axis=1, tiled=True)
    normed_rows = rms_scale(full_rows.astype(jnp.float32), latent_gain.astype(jnp.float32)).astype(
        jnp.bfloat16
    )
    inner_width = lat_qkv.shape[2]
    projected = jnp.einsum(
        "pd,idc->ipc",
        normed_rows,
        lax.all_gather(lat_qkv, "seq", axis=1, tiled=True),
        preferred_element_type=jnp.float32,
    )
    heads_here = inner_width // HD
    queries = rotate(projected[0].reshape(slot_total, heads_here, HD), position).astype(
        jnp.bfloat16
    )
    latent_keys = (
        rotate(projected[1].reshape(slot_total, heads_here, HD), position)
        .astype(jnp.bfloat16)
        .reshape(slot_total, inner_width)
    )
    latent_values = projected[2].astype(jnp.bfloat16)
    latent_pos = jnp.where(in_use, position, far_position)
    largest = jnp.full((heads_here, slot_total), -1e30, jnp.float32)
    piece_keys = lax.all_gather(latent_keys, "seq", axis=0, tiled=True)
    piece_values = lax.all_gather(latent_values, "seq", axis=0, tiled=True)
    piece_pos = lax.all_gather(shortened(latent_pos), "seq", axis=0, tiled=True)
    rows_here = piece_keys.shape[0]
    piece_scores = jnp.einsum(
        "qhd,khd->hqk",
        queries,
        piece_keys.reshape(rows_here, heads_here, HD),
        preferred_element_type=jnp.float32,
    ) * (1.0 / math.sqrt(HD))
    permitted = (piece_pos[None, :] <= position[:, None])[None]
    piece_scores = jnp.where(permitted, piece_scores, -1e30)
    renewed = jnp.maximum(largest, jnp.max(piece_scores, axis=-1))
    raised = jnp.where(permitted, jnp.exp(piece_scores - renewed[..., None]), 0.0)
    weight_sum = jnp.sum(raised, axis=-1)
    weighted = jnp.einsum(
        "hqk,khd->hqd",
        raised.astype(jnp.bfloat16),
        piece_values.reshape(rows_here, heads_here, HD),
        preferred_element_type=jnp.float32,
    )
    largest, weight_sum, weighted = (renewed, weight_sum, weighted)
    latent_heads = (
        (weighted / weight_sum[..., None])
        .transpose(1, 0, 2)
        .reshape(slot_total, inner_width)
        .astype(jnp.bfloat16)
    )
    partials = jnp.dot(
        latent_heads,
        lax.all_gather(lat_proj_out, "seq", axis=1, tiled=True),
        preferred_element_type=jnp.float32,
    )
    reduced = lax.psum_scatter(partials, "tp", scatter_dimension=1, tiled=True)
    latent = jnp.where(in_use[:, None], patches.astype(jnp.float32) + reduced, 0.0).astype(
        jnp.bfloat16
    )
    return (encoded, latent)


def solution(mesh):
    return jax.shard_map(
        shards,
        mesh=mesh,
        in_specs=(
            P("seq", None),
            P(),
            P(None, None, "tp"),
            P("tp", None),
            P("seq", None),
            P("seq"),
            P(None, "tp"),
            P(None, None, "tp"),
            P(),
            P(None, "seq", "tp"),
            P("tp", "seq"),
        ),
        out_specs=(P("seq", None), P("seq", "tp")),
        check_vma=False,
    )
```

profile of v0, /device:TPU:0, one launch (start us, length us, event | category | flops | bytes accessed | tf_op | source)
XLA Modules:
  0.0 188.4 jit_solution(6038080020906645445)
XLA Ops:
  10.1 2.4 %fusion.30 = bf16[3,256,256]{1,2,0:T(8,128)(2,1)S(1)} fusion(bf16[3,1024,256]{2,1,0:T(8,128)(2,1)} %param.15, bf16[256,1024]{1,0:T(8,128)(2,1)} %param.13, f32[1024]{0:T(1024)S(1)} %convert_element_type.99, f32[256]{0:T(256)S(1)} %add_rsqrt_fusion), kind=kOutput, calls=%fused_computation.34 | convolution fusion | flops 403898368 | bytes 2495488 | tf_op jit(solution)/shard_map/bd,idc->ibc/dot_general | solution.py:133
  12.5 4.9 %collective-permute-start.2 = (bf16[256,256]{0,1:T(8,128)(2,1)S(1)}, bf16[256,256]{0,1:T(8,128)(2,1)S(1)}, u32[]{:S(2)}, u32[]{:S(2)}) collective-permute-start(bf16[256,256]{0,1:T(8,128)(2,1)S(1)} %get-tuple-element.93), channel_id=1, source_target_pairs={{0,8},{4,12},{8,16},{12,20},{16,24},{20,28},{1,9},{5,13},{9,17},{1... | collective-permute-start | bytes 393224 | tf_op jit(solution)/shard_map/ppermute | solution.py:19
  17.4 1.5 collective-permute-start.3
  18.9 3.9 %collective-permute-start = (bf16[256,256]{0,1:T(8,128)(2,1)S(1)}, bf16[256,256]{0,1:T(8,128)(2,1)S(1)}, u32[]{:S(2)}, u32[]{:S(2)}) collective-permute-start(bf16[256,256]{0,1:T(8,128)(2,1)S(1)} %get-tuple-element.92), channel_id=1, source_target_pairs={{0,8},{4,12},{8,16},{12,20},{16,24},{20,28},{1,9},{5,13},{9,17},{1... | collective-permute-start | bytes 393224 | tf_op jit(solution)/shard_map/ppermute | solution.py:19
  22.8 3.2 %collective-permute-start.1 = (bf16[256,256]{0,1:T(8,128)(2,1)S(1)}, bf16[256,256]{0,1:T(8,128)(2,1)S(1)}, u32[]{:S(2)}, u32[]{:S(2)}) collective-permute-start(bf16[256,256]{0,1:T(8,128)(2,1)S(1)} %get-tuple-element.92), channel_id=1, source_target_pairs={{0,4},{4,8},{8,12},{12,16},{16,20},{20,24},{24,28},{1,5},{5,9},{9,... | collective-permute-start | bytes 393224 | tf_op jit(solution)/shard_map/ppermute | solution.py:19
  26.9 1.8 fusion.112
  29.8 1.4 fusion.119
  35.3 9.8 %all-reduce = s32[8]{0:T(128)S(1)} all-reduce(s32[8]{0:T(128)S(1)} %dynamic-update-slice), channel_id=2, replica_groups=mesh['seq'=8,'tp'=4] {'seq'}, use_global_device_ids=true, to_apply=%add | all-reduce | flops 8 | bytes 64
  45.1 8.7 %while.13 = (s32[]{:T(128)}, s32[1]{0:T(128)}, s32[]{:T(128)}, s32[8,1]{0,1:T(1,128)S(1)}, s32[]{:T(128)}) while((s32[]{:T(128)}, s32[1]{0:T(128)}, s32[]{:T(128)}, s32[8,1]{0,1:T(1,128)S(1)}, s32[]{:T(128)}) %tuple.59), condition=%wide.region_8.9_spmd, body=%wide.region_7.8_spmd.sunk | while | flops 5 | bytes 107 | solution.py:31
  54.6 7.3 %all-reduce.1 = s32[512]{0:T(512)S(1)} all-reduce(s32[512]{0:T(512)S(1)} %select_dynamic-update-slice_fusion), channel_id=1, replica_groups=mesh['seq'=8,'tp'=4] {'seq'}, use_global_device_ids=true, to_apply=%add.1 | all-reduce | flops 512 | bytes 4096
  63.3 20.8 %all-reduce.4.cloned.1.call-done = f32[256,1024]{1,0:T(8,128)} async-done(((f32[256,1024]{1,0:T(8,128)}), f32[256,1024]{1,0:T(8,128)}) %all-reduce.4.cloned.1.call-update) | async-done | bytes 1048592 | tf_op jit(solution)/shard_map/psum | solution.py:172
  84.2 1.4 fusion.43
  86.9 1.8 collective-permute-done.5
  88.7 3.1 %fusion.23 = bf16[33,8,8,128]{3,2,1,0:T(8,128)(2,1)} fusion(bf16[2,1024,1024]{2,1,0:T(8,128)(2,1)} %param.20, bf16[8,1024]{1,0:T(8,128)(2,1)S(1)} %collective-permute-done.5, bf16[256,1024]{1,0:T(8,128)(2,1)S(1)} %fusion.43), kind=kOutput, calls=%fused_computation.30 | convolution fusion | flops 554999808 | bytes 3178496 | tf_op jit(solution)/shard_map/dot_general | solution.py:85
  92.5 2.5 %fusion.113 = (f32[8,64]{1,0:T(8,128)S(1)}, f32[8,64,264]{2,1,0:T(8,128)}) fusion(bf16[33,8,8,128]{3,2,1,0:T(8,128)(2,1)} %fusion.23, pred[64,264]{1,0:T(8,128)(4,1)S(1)} %and_or_fusion, f32[64,1024]{1,0:T(8,128)S(1)} %fusion.33), kind=kOutput, calls=%fused_computation.147 | convolution fusion | flops 35344648 | bytes 1362432 | tf_op jit(solution)/shard_map/sub | solution.py:50
  95.0 2.4 %fusion.26 = bf16[33,8,8,128]{3,2,1,0:T(8,128)(2,1)S(1)} fusion(bf16[2,1024,1024]{2,1,0:T(8,128)(2,1)} %param.20, bf16[8,1024]{1,0:T(8,128)(2,1)S(1)} %collective-permute-done.5, bf16[256,1024]{1,0:T(8,128)(2,1)S(1)} %fusion.43), kind=kOutput, calls=%fused_computation.31 | convolution fusion | flops 554999808 | bytes 3178496 | tf_op jit(solution)/shard_map/dot_general | solution.py:88
  97.8 15.5 %all_gather.27 = bf16[64,4096]{1,0:T(8,128)(2,1)S(1)} all-gather(bf16[64,1024]{1,0:T(8,128)(2,1)S(1)} %fusion.73), channel_id=1, replica_groups=mesh['seq'=8,'tp'=4] {'tp'}, dimensions={1}, use_global_device_ids=true | all-gather | bytes 655360 | tf_op jit(solution)/shard_map/all_gather | solution.py:188
  113.5 7.5 %convolution_bitcast_fusion = f32[3,64,512]{2,1,0:T(8,128)S(1)} fusion(bf16[3,4096,512]{2,1,0:T(8,128)(2,1)} %all-gather.5.cloned.1.call-done, bf16[64,4096]{1,0:T(8,128)(2,1)S(1)} %all_gather.27, f32[4096]{0:T(1024)S(1)} %convert_element_type.118, f32[64]{0:T(128)S(1)} %add_rsqrt_fusion.1), kind=kOutput, calls=%fused_computation.35 | convolution fusion | flops 806354944 | bytes 13517056 | tf_op jit(solution)/shard_map/pd,idc->ipc/dot_general | solution.py:193
  121.6 11.9 %all_gather.29 = bf16[512,512]{1,0:T(8,128)(2,1)S(1)} all-gather(bf16[64,512]{1,0:T(8,128)(2,1)S(1)} %copy_bitcast_fusion), channel_id=1, replica_groups=mesh['seq'=8,'tp'=4] {'seq'}, dimensions={0}, use_global_device_ids=true | all-gather | bytes 589824 | tf_op jit(solution)/shard_map/all_gather | solution.py:211
  133.7 11.9 %all-gather.1 = bf16[1,512,512]{2,1,0:T(8,128)(2,1)S(1)} all-gather(bf16[1,64,512]{2,1,0:T(8,128)(2,1)S(1)} %slice.101), channel_id=3, replica_groups=mesh['seq'=8,'tp'=4] {'seq'}, dimensions={1}, use_global_device_ids=true | all-gather | bytes 589824 | tf_op jit(solution)/shard_map/all_gather | solution.py:212
  147.1 1.3 fusion.36
  148.5 4.0 %fusion.80 = f32[64,4096]{1,0:T(8,128)} fusion(bf16[512,4096]{1,0:T(8,128)(2,1)} %all-gather.7.cloned.1.call-done, bf16[4,8,8,128]{3,2,1,0:T(8,128)(2,1)S(1)} %fusion.36), kind=kOutput, calls=%fused_computation.100 | convolution fusion | flops 268435456 | bytes 5308416 | tf_op jit(solution)/shard_map/dot_general | solution.py:239
  152.6 26.7 %reduce-scatter.2.cloned.1.call-done = f32[64,1024]{1,0:T(8,128)} async-done(((f32[64,4096]{1,0:T(8,128)}), f32[64,1024]{1,0:T(8,128)}) %reduce-scatter.2.cloned.1.call-update) | async-done | bytes 262160 | tf_op jit(solution)/shard_map/reduce_scatter | solution.py:244
  179.3 1.7 select_convert_fusion
  (89 shorter events, 17.3 us)
Async XLA Ops:
  8.0 83.8 %copy-start = (bf16[1024,1024]{1,0:T(8,128)(2,1)S(1)}, bf16[1024,1024]{1,0:T(8,128)(2,1)}, u32[]{:S(2)}) copy-start(bf16[1024,1024]{1,0:T(8,128)(2,1)} %param.19) | copy-start | bytes 6291460
  8.0 76.1 %all-reduce.4.cloned.1.call-start = ((), (), s32[]{:S(2)}) async-start(), calls=%async_computation.1 | async-start | bytes 2097152 | tf_op jit(solution)/shard_map/psum | solution.py:172
  12.5 13.8 %collective-permute-start.2 = (bf16[256,256]{0,1:T(8,128)(2,1)S(1)}, bf16[256,256]{0,1:T(8,128)(2,1)S(1)}, u32[]{:S(2)}, u32[]{:S(2)}) collective-permute-start(bf16[256,256]{0,1:T(8,128)(2,1)S(1)} %get-tuple-element.93), channel_id=1, source_target_pairs={{0,8},{4,12},{8,16},{12,20},{16,24},{20,28},{1,9},{5,13},{9,17},{1... | collective-permute-start | bytes 393224 | tf_op jit(solution)/shard_map/ppermute | solution.py:19
  17.4 8.9 %collective-permute-start.3 = (bf16[256,256]{0,1:T(8,128)(2,1)S(1)}, bf16[256,256]{0,1:T(8,128)(2,1)S(1)}, u32[]{:S(2)}, u32[]{:S(2)}) collective-permute-start(bf16[256,256]{0,1:T(8,128)(2,1)S(1)} %get-tuple-element.93), channel_id=1, source_target_pairs={{0,4},{4,8},{8,12},{12,16},{16,20},{20,24},{24,28},{1,5},{5,9},{9,... | collective-permute-start | bytes 393224 | tf_op jit(solution)/shard_map/ppermute | solution.py:19
  18.9 9.9 %collective-permute-start = (bf16[256,256]{0,1:T(8,128)(2,1)S(1)}, bf16[256,256]{0,1:T(8,128)(2,1)S(1)}, u32[]{:S(2)}, u32[]{:S(2)}) collective-permute-start(bf16[256,256]{0,1:T(8,128)(2,1)S(1)} %get-tuple-element.92), channel_id=1, source_target_pairs={{0,8},{4,12},{8,16},{12,20},{16,24},{20,28},{1,9},{5,13},{9,17},{1... | collective-permute-start | bytes 393224 | tf_op jit(solution)/shard_map/ppermute | solution.py:19
  22.8 6.0 %collective-permute-start.1 = (bf16[256,256]{0,1:T(8,128)(2,1)S(1)}, bf16[256,256]{0,1:T(8,128)(2,1)S(1)}, u32[]{:S(2)}, u32[]{:S(2)}) collective-permute-start(bf16[256,256]{0,1:T(8,128)(2,1)S(1)} %get-tuple-element.92), channel_id=1, source_target_pairs={{0,4},{4,8},{8,12},{12,16},{16,20},{20,24},{24,28},{1,5},{5,9},{9,... | collective-permute-start | bytes 393224 | tf_op jit(solution)/shard_map/ppermute | solution.py:19
  28.8 1.0 copy-start.3
  29.5 2.3 %copy-start.5 = (s32[1,64]{1,0:T(1,128)S(1)}, s32[1,64]{1,0:T(1,128)}, u32[]{:S(2)}) copy-start(s32[1,64]{1,0:T(1,128)} %param.17) | copy-start | bytes 772
  29.5 4.4 %copy-start.6 = (u32[32]{0:T(128)S(1)}, u32[32]{0:T(128)}, u32[]{:S(2)}) copy-start(u32[32]{0:T(128)} %constant.80) | copy-start | bytes 388
  29.5 25.0 %copy-start.4 = (bf16[4096]{0:T(1024)(128)(2,1)S(1)}, bf16[4096]{0:T(1024)(128)(2,1)}, u32[]{:S(2)}) copy-start(bf16[4096]{0:T(1024)(128)(2,1)} %param.21) | copy-start | bytes 24580
  29.5 54.6 %copy-start.1 = (bf16[256,1024]{1,0:T(8,128)(2,1)S(1)}, bf16[256,1024]{1,0:T(8,128)(2,1)}, u32[]{:S(2)}) copy-start(bf16[256,1024]{1,0:T(8,128)(2,1)} %param.13) | copy-start | bytes 1572868
  31.2 82.3 %all-gather.5.cloned.1.call-start = ((), (), s32[]{:S(2)}) async-start(), calls=%async_computation.2 | async-start | bytes 14155776 | tf_op jit(solution)/shard_map/all_gather | solution.py:196
  31.8 116.7 %all-gather.7.cloned.1.call-start = ((), (), s32[]{:S(2)}) async-start(), calls=%async_computation.3 | async-start | bytes 4718592 | tf_op jit(solution)/shard_map/all_gather | solution.py:241
  31.9 30.4 %collective-permute-start.4 = (bf16[1]{0:T(256)(128)(2,1)}, bf16[1]{0:T(256)(128)(2,1)}, u32[]{:S(2)}, u32[]{:S(2)}) collective-permute-start(bf16[1]{0:T(256)(128)(2,1)} %convert_element_type.108), channel_id=1, source_target_pairs={{4,0},{8,4},{12,8},{16,12},{20,16},{24,20},{28,24},{5,1},{9,5},{13... | collective-permute-start | bytes 14 | tf_op jit(solution)/shard_map/ppermute | solution.py:19
  33.2 146.0 %reduce-scatter.2.cloned.1.call-start = ((), (), s32[]{:S(2)}) async-start(), calls=%async_computation.4 | async-start | bytes 1310720 | tf_op jit(solution)/shard_map/reduce_scatter | solution.py:244
  85.5 9.4 %copy-start.2 = (bf16[256,1024]{1,0:T(8,128)(2,1)}, bf16[256,1024]{1,0:T(8,128)(2,1)S(1)}, u32[]{:S(2)}) copy-start(bf16[256,1024]{1,0:T(8,128)(2,1)S(1)} %fusion.43) | copy-start | bytes 1572868
  85.6 3.1 %collective-permute-start.5 = (bf16[8,1024]{1,0:T(8,128)(2,1)S(1)}, bf16[8,1024]{1,0:T(8,128)(2,1)S(1)}, u32[]{:S(2)}, u32[]{:S(2)}) collective-permute-start(bf16[8,1024]{1,0:T(8,128)(2,1)S(1)} %slice.73), channel_id=1, source_target_pairs={{4,0},{8,4},{12,8},{16,12},{20,16},{24,20},{28,24},{5,1},{9,5},{13... | collective-permute-start | bytes 49160 | tf_op jit(solution)/shard_map/ppermute | solution.py:19
  95.0 2.4 %copy-start.7 = (f32[8,64,264]{2,1,0:T(8,128)S(1)}, f32[8,64,264]{2,1,0:T(8,128)}, u32[]{:S(2)}) copy-start(f32[8,64,264]{2,1,0:T(8,128)} %get-tuple-element.112) | copy-start | bytes 1622020
Sparse Core Ops, SparseCore 0:
  31.3 52.7 all-reduce.3
  152.7 26.5 reduce-scatter.1
Sparse Core Ops, SparseCore 1:
  33.6 72.8 all-gather.4
  108.2 39.8 all-gather.6
where the time goes:
time: 189 us; the launch traced here: 188 us
  blocking collectives  56.4 us (30%)
  waiting for transfers between devices  50 us (26%)
  matrix products  27.2 us (14%)
  between operations  17.9 us (9%)
  starting transfers between devices  16.2 us (9%)
  other arithmetic  8.76 us (5%)
  local copies, waits for them, and re-layouts  7.47 us (4%)
  loops' own time  4.55 us (2%)
    reduce_scatter x1, waiting for transfers between devices, shards(): reduced = lax.psum_scatter(partials, 'tp', scatter_dimension=1, tiled=True)  26.7 us
    psum x1, waiting for transfers between devices, shards(): lax.psum(jnp.dot(attended, enc_proj_out, preferred_element_type=jnp.float...  20.8 us
    unnamed x2, blocking collectives  17.1 us
    ppermute x6, starting transfers between devices, from_behind(): lax.ppermute(value, axis, [(source, source + steps) for source in range(l...  16 us
    all_gather x1, blocking collectives, shards(): full_rows = lax.all_gather(patches, 'tp', axis=1, tiled=True)  15.5 us
    all_gather x1, blocking collectives, shards(): piece_keys = lax.all_gather(latent_keys, 'seq', axis=0, tiled=True)  11.9 us
    all_gather x1, blocking collectives, shards(): piece_values = lax.all_gather(latent_values, 'seq', axis=0, tiled=True)  11.9 us
    dot_general x1, matrix products, shards(): jnp.einsum('pd,idc->ipc', normed_rows, lax.all_gather(lat_qkv, 'seq', axi...  7.47 us
  transfers between devices with their start and end apart: 10, of which 3 were waited for; matrix products, arithmetic and copies ran while one was open for 16% of the time, Pallas kernels for 0%

commit v1 on v0

--- a/solution.py
+++ b/solution.py
@@ -169,7 +169,10 @@
         preferred_element_type=jnp.float32,
     )
     attended = attended.reshape(byte_rows, head_count * EH).astype(jnp.bfloat16)
-    blended = lax.psum(jnp.dot(attended, enc_proj_out, preferred_element_type=jnp.float32), "tp")
+    blended = jnp.sum(
+        lax.all_gather(jnp.dot(attended, enc_proj_out, preferred_element_type=jnp.float32), "tp"),
+        axis=0,
+    )
     encoded = (states + blended).astype(jnp.bfloat16)
     patch_count = counts[0]
     local_starts = starts[0]

time: 189 us -> 267 us (1.41)
  waiting for transfers between devices: 50 us -> 126 us
  other arithmetic: 8.76 us -> 11.9 us
    all_gather x0 -> x1, waiting for transfers between devices: none -> 49.2 us  [shards(): lax.all_gather(jnp.dot(attended, enc_proj_out, preferred_element_type=jnp...]
    all_gather x1, waiting for transfers between devices: 0.02 us -> 38.6 us  [shards(): lax.all_gather(lat_qkv, 'seq', axis=1, tiled=True)]
    psum x1 -> x0, waiting for transfers between devices: 20.8 us -> none  [shards(): lax.psum(jnp.dot(attended, enc_proj_out, preferred_element_type=jnp.float...]
    all_gather x1, waiting for transfers between devices: 0.03 us -> 8.75 us  [shards(): lax.all_gather(lat_proj_out, 'seq', axis=1, tiled=True)]
    reduce_sum x0 -> x1, other arithmetic: none -> 2.72 us  [shards(): jnp.sum(lax.all_gather(jnp.dot(attended, enc_proj_out, preferred_element_...]
  transfers between devices with their start and end apart: 10 -> 10, of which waited for: 3 -> 5; matrix products, arithmetic and copies ran while one was open for 16% -> 13% of each run, Pallas kernels for 0% -> 0%
where the time goes in v1:
time: 267 us; the launch traced here: 266 us
  waiting for transfers between devices  126 us (47%)
  blocking collectives  55 us (21%)
  matrix products  28.1 us (11%)
  starting transfers between devices  16.2 us (6%)
  between operations  16.2 us (6%)
  other arithmetic  11.9 us (4%)
  local copies, waits for them, and re-layouts  7.59 us (3%)
  loops' own time  4.48 us (2%)
    all_gather x1, waiting for transfers between devices, shards(): lax.all_gather(jnp.dot(attended, enc_proj_out, preferred_element_type=jnp...  49.2 us
    all_gather x1, waiting for transfers between devices, shards(): lax.all_gather(lat_qkv, 'seq', axis=1, tiled=True)  38.6 us
    reduce_scatter x1, waiting for transfers between devices, shards(): reduced = lax.psum_scatter(partials, 'tp', scatter_dimension=1, tiled=True)  27.4 us
    unnamed x2, blocking collectives  16.7 us
    ppermute x6, starting transfers between devices, from_behind(): lax.ppermute(value, axis, [(source, source + steps) for source in range(l...  16 us
    all_gather x1, blocking collectives, shards(): full_rows = lax.all_gather(patches, 'tp', axis=1, tiled=True)  16 us
    all_gather x1, blocking collectives, shards(): piece_keys = lax.all_gather(latent_keys, 'seq', axis=0, tiled=True)  12.5 us
    all_gather x1, blocking collectives, shards(): piece_values = lax.all_gather(latent_values, 'seq', axis=0, tiled=True)  9.83 us
  transfers between devices with their start and end apart: 10, of which 5 were waited for; matrix products, arithmetic and copies ran while one was open for 13% of the time, Pallas kernels for 0%

profile of v1, /device:TPU:0, one launch (start us, length us, event | category | flops | bytes accessed | tf_op | source)
XLA Modules:
  0.0 265.9 jit_solution(11503046220116922477)
XLA Ops:
  9.3 2.4 fusion.30
  11.7 4.9 %collective-permute-start.2 = (bf16[256,256]{0,1:T(8,128)(2,1)S(1)}, bf16[256,256]{0,1:T(8,128)(2,1)S(1)}, u32[]{:S(2)}, u32[]{:S(2)}) collective-permute-start(bf16[256,256]{0,1:T(8,128)(2,1)S(1)} %get-tuple-element.93), channel_id=1, source_target_pairs={{0,8},{4,12},{8,16},{12,20},{16,24},{20,28},{1,9},{5,13},{9,17},{1... | collective-permute-start | bytes 393224 | tf_op jit(solution)/shard_map/ppermute | solution.py:19
  18.1 3.9 %collective-permute-start = (bf16[256,256]{0,1:T(8,128)(2,1)S(1)}, bf16[256,256]{0,1:T(8,128)(2,1)S(1)}, u32[]{:S(2)}, u32[]{:S(2)}) collective-permute-start(bf16[256,256]{0,1:T(8,128)(2,1)S(1)} %get-tuple-element.92), channel_id=1, source_target_pairs={{0,8},{4,12},{8,16},{12,20},{16,24},{20,28},{1,9},{5,13},{9,17},{1... | collective-permute-start | bytes 393224 | tf_op jit(solution)/shard_map/ppermute | solution.py:19
  21.9 3.2 %collective-permute-start.1 = (bf16[256,256]{0,1:T(8,128)(2,1)S(1)}, bf16[256,256]{0,1:T(8,128)(2,1)S(1)}, u32[]{:S(2)}, u32[]{:S(2)}) collective-permute-start(bf16[256,256]{0,1:T(8,128)(2,1)S(1)} %get-tuple-element.92), channel_id=1, source_target_pairs={{0,4},{4,8},{8,12},{12,16},{16,20},{20,24},{24,28},{1,5},{5,9},{9,... | collective-permute-start | bytes 393224 | tf_op jit(solution)/shard_map/ppermute | solution.py:19
  26.1 1.8 fusion.112
  34.7 9.8 %all-reduce = s32[8]{0:T(128)S(1)} all-reduce(s32[8]{0:T(128)S(1)} %dynamic-update-slice), channel_id=3, replica_groups=mesh['seq'=8,'tp'=4] {'seq'}, use_global_device_ids=true, to_apply=%add | all-reduce | flops 8 | bytes 64
  44.5 8.6 %while.13 = (s32[]{:T(128)}, s32[1]{0:T(128)}, s32[]{:T(128)}, s32[8,1]{0,1:T(1,128)S(1)}, s32[]{:T(128)}) while((s32[]{:T(128)}, s32[1]{0:T(128)}, s32[]{:T(128)}, s32[8,1]{0,1:T(1,128)S(1)}, s32[]{:T(128)}) %tuple.59), condition=%wide.region_8.9_spmd, body=%wide.region_7.8_spmd.sunk | while | flops 5 | bytes 107 | solution.py:31
  53.9 6.9 %all-reduce.1 = s32[512]{0:T(512)S(1)} all-reduce(s32[512]{0:T(512)S(1)} %select_dynamic-update-slice_fusion), channel_id=1, replica_groups=mesh['seq'=8,'tp'=4] {'seq'}, use_global_device_ids=true, to_apply=%add.1 | all-reduce | flops 512 | bytes 4096
  62.9 49.2 %all-gather.11.cloned.1.call-done = f32[1024,1024]{1,0:T(8,128)} async-done(((f32[256,1024]{1,0:T(8,128)}), f32[1024,1024]{1,0:T(8,128)}) %all-gather.11.cloned.1.call-update) | async-done | bytes 4194320 | tf_op jit(solution)/shard_map/all_gather | solution.py:173
  112.1 2.7 %reduce_sum.65 = f32[256,1024]{1,0:T(8,128)S(1)} reduce(f32[4,256,1024]{2,1,0:T(8,128)} %bitcast.129, f32[]{:T(128)} %constant.31.clone.1), dimensions={0}, to_apply=%region_3.4 | reduce | flops 786432 | bytes 5242884 | tf_op jit(solution)/shard_map/reduce_sum | solution.py:172
  117.4 1.8 collective-permute-done.5
  119.1 3.5 %fusion.23 = bf16[33,8,8,128]{3,2,1,0:T(8,128)(2,1)} fusion(bf16[2,1024,1024]{2,1,0:T(8,128)(2,1)} %param.20, bf16[8,1024]{1,0:T(8,128)(2,1)S(1)} %collective-permute-done.5, bf16[256,1024]{1,0:T(8,128)(2,1)S(1)} %fusion.43), kind=kOutput, calls=%fused_computation.30 | convolution fusion | flops 554999808 | bytes 3178496 | tf_op jit(solution)/shard_map/dot_general | solution.py:85
  122.6 1.9 fusion.33
  124.5 2.4 fusion.113
  126.9 2.4 fusion.26
  129.7 16.0 %all_gather.35 = bf16[64,4096]{1,0:T(8,128)(2,1)S(1)} all-gather(bf16[64,1024]{1,0:T(8,128)(2,1)S(1)} %fusion.73), channel_id=1, replica_groups=mesh['seq'=8,'tp'=4] {'tp'}, dimensions={1}, use_global_device_ids=true | all-gather | bytes 655360 | tf_op jit(solution)/shard_map/all_gather | solution.py:191
  146.0 38.6 %all-gather.7.cloned.1.call-done = bf16[3,4096,512]{2,1,0:T(8,128)(2,1)} async-done(((bf16[3,512,512]{2,1,0:T(8,128)(2,1)}), bf16[3,4096,512]{2,1,0:T(8,128)(2,1)}) %all-gather.7.cloned.1.call-update) | async-done | bytes 12582928 | tf_op jit(solution)/shard_map/all_gather | solution.py:199
  184.5 6.9 %convolution_bitcast_fusion = f32[3,64,512]{2,1,0:T(8,128)S(1)} fusion(bf16[3,4096,512]{2,1,0:T(8,128)(2,1)} %all-gather.7.cloned.1.call-done, bf16[64,4096]{1,0:T(8,128)(2,1)S(1)} %all_gather.35, f32[4096]{0:T(1024)S(1)} %convert_element_type.118, f32[64]{0:T(128)S(1)} %add_rsqrt_fusion.1), kind=kOutput, calls=%fused_computation.35 | convolution fusion | flops 806354944 | bytes 13517056 | tf_op jit(solution)/shard_map/pd,idc->ipc/dot_general | solution.py:196
  192.1 12.5 %all_gather.37 = bf16[512,512]{1,0:T(8,128)(2,1)S(1)} all-gather(bf16[64,512]{1,0:T(8,128)(2,1)S(1)} %copy_bitcast_fusion), channel_id=1, replica_groups=mesh['seq'=8,'tp'=4] {'seq'}, dimensions={0}, use_global_device_ids=true | all-gather | bytes 589824 | tf_op jit(solution)/shard_map/all_gather | solution.py:214
  204.8 9.8 %all-gather.2 = bf16[1,512,512]{2,1,0:T(8,128)(2,1)S(1)} all-gather(bf16[1,64,512]{2,1,0:T(8,128)(2,1)S(1)} %slice.101), channel_id=4, replica_groups=mesh['seq'=8,'tp'=4] {'seq'}, dimensions={1}, use_global_device_ids=true | all-gather | bytes 589824 | tf_op jit(solution)/shard_map/all_gather | solution.py:215
  217.5 8.8 %all-gather.9.cloned.1.call-done = bf16[512,4096]{1,0:T(8,128)(2,1)} async-done(((bf16[512,512]{1,0:T(8,128)(2,1)}), bf16[512,4096]{1,0:T(8,128)(2,1)}) %all-gather.9.cloned.1.call-update) | async-done | bytes 4194320 | tf_op jit(solution)/shard_map/all_gather | solution.py:244
  226.2 4.0 %fusion.80 = f32[64,4096]{1,0:T(8,128)} fusion(bf16[512,4096]{1,0:T(8,128)(2,1)} %all-gather.9.cloned.1.call-done, bf16[4,8,8,128]{3,2,1,0:T(8,128)(2,1)S(1)} %fusion.36), kind=kOutput, calls=%fused_computation.100 | convolution fusion | flops 268435456 | bytes 5308416 | tf_op jit(solution)/shard_map/dot_general | solution.py:242
  230.3 27.4 %reduce-scatter.2.cloned.1.call-done = f32[64,1024]{1,0:T(8,128)} async-done(((f32[64,4096]{1,0:T(8,128)}), f32[64,1024]{1,0:T(8,128)}) %reduce-scatter.2.cloned.1.call-update) | async-done | bytes 262160 | tf_op jit(solution)/shard_map/reduce_scatter | solution.py:247
  257.7 1.7 select_convert_fusion
  (92 shorter events, 22.8 us)
Async XLA Ops:
  7.2 115.5 %copy-start = (bf16[1024,1024]{1,0:T(8,128)(2,1)S(1)}, bf16[1024,1024]{1,0:T(8,128)(2,1)}, u32[]{:S(2)}) copy-start(bf16[1024,1024]{1,0:T(8,128)(2,1)} %param.19) | copy-start | bytes 6291460
  7.2 104.9 %all-gather.11.cloned.1.call-start = ((), (), s32[]{:S(2)}) async-start(), calls=%async_computation.4 | async-start | bytes 5242880 | tf_op jit(solution)/shard_map/all_gather | solution.py:173
  11.7 13.8 %collective-permute-start.2 = (bf16[256,256]{0,1:T(8,128)(2,1)S(1)}, bf16[256,256]{0,1:T(8,128)(2,1)S(1)}, u32[]{:S(2)}, u32[]{:S(2)}) collective-permute-start(bf16[256,256]{0,1:T(8,128)(2,1)S(1)} %get-tuple-element.93), channel_id=1, source_target_pairs={{0,8},{4,12},{8,16},{12,20},{16,24},{20,28},{1,9},{5,13},{9,17},{1... | collective-permute-start | bytes 393224 | tf_op jit(solution)/shard_map/ppermute | solution.py:19
  16.6 8.9 %collective-permute-start.3 = (bf16[256,256]{0,1:T(8,128)(2,1)S(1)}, bf16[256,256]{0,1:T(8,128)(2,1)S(1)}, u32[]{:S(2)}, u32[]{:S(2)}) collective-permute-start(bf16[256,256]{0,1:T(8,128)(2,1)S(1)} %get-tuple-element.93), channel_id=1, source_target_pairs={{0,4},{4,8},{8,12},{12,16},{16,20},{20,24},{24,28},{1,5},{5,9},{9,... | collective-permute-start | bytes 393224 | tf_op jit(solution)/shard_map/ppermute | solution.py:19
  18.1 9.9 %collective-permute-start = (bf16[256,256]{0,1:T(8,128)(2,1)S(1)}, bf16[256,256]{0,1:T(8,128)(2,1)S(1)}, u32[]{:S(2)}, u32[]{:S(2)}) collective-permute-start(bf16[256,256]{0,1:T(8,128)(2,1)S(1)} %get-tuple-element.92), channel_id=1, source_target_pairs={{0,8},{4,12},{8,16},{12,20},{16,24},{20,28},{1,9},{5,13},{9,17},{1... | collective-permute-start | bytes 393224 | tf_op jit(solution)/shard_map/ppermute | solution.py:19
  21.9 6.0 %collective-permute-start.1 = (bf16[256,256]{0,1:T(8,128)(2,1)S(1)}, bf16[256,256]{0,1:T(8,128)(2,1)S(1)}, u32[]{:S(2)}, u32[]{:S(2)}) collective-permute-start(bf16[256,256]{0,1:T(8,128)(2,1)S(1)} %get-tuple-element.92), channel_id=1, source_target_pairs={{0,4},{4,8},{8,12},{12,16},{16,20},{20,24},{24,28},{1,5},{5,9},{9,... | collective-permute-start | bytes 393224 | tf_op jit(solution)/shard_map/ppermute | solution.py:19
  28.0 1.0 copy-start.3
  28.7 2.5 copy-start.6
  28.7 4.5 %copy-start.7 = (u32[32]{0:T(128)S(1)}, u32[32]{0:T(128)}, u32[]{:S(2)}) copy-start(u32[32]{0:T(128)} %constant.80) | copy-start | bytes 388
  28.7 25.3 %copy-start.5 = (bf16[4096]{0:T(1024)(128)(2,1)S(1)}, bf16[4096]{0:T(1024)(128)(2,1)}, u32[]{:S(2)}) copy-start(bf16[4096]{0:T(1024)(128)(2,1)} %param.21) | copy-start | bytes 24580
  30.3 154.2 %all-gather.7.cloned.1.call-start = ((), (), s32[]{:S(2)}) async-start(), calls=%async_computation.1 | async-start | bytes 14155776 | tf_op jit(solution)/shard_map/all_gather | solution.py:199
  31.1 195.2 %all-gather.9.cloned.1.call-start = ((), (), s32[]{:S(2)}) async-start(), calls=%async_computation.2 | async-start | bytes 4718592 | tf_op jit(solution)/shard_map/all_gather | solution.py:244
  31.2 30.7 %collective-permute-start.4 = (bf16[1]{0:T(256)(128)(2,1)}, bf16[1]{0:T(256)(128)(2,1)}, u32[]{:S(2)}, u32[]{:S(2)}) collective-permute-start(bf16[1]{0:T(256)(128)(2,1)} %convert_element_type.108), channel_id=1, source_target_pairs={{4,0},{8,4},{12,8},{16,12},{20,16},{24,20},{28,24},{5,1},{9,5},{13... | collective-permute-start | bytes 14 | tf_op jit(solution)/shard_map/ppermute | solution.py:19
  32.5 225.2 %reduce-scatter.2.cloned.1.call-start = ((), (), s32[]{:S(2)}) async-start(), calls=%async_computation.3 | async-start | bytes 1310720 | tf_op jit(solution)/shard_map/reduce_scatter | solution.py:247
  116.0 3.1 %copy-start.1 = (bf16[256,1024]{1,0:T(8,128)(2,1)}, bf16[256,1024]{1,0:T(8,128)(2,1)S(1)}, u32[]{:S(2)}) copy-start(bf16[256,1024]{1,0:T(8,128)(2,1)S(1)} %fusion.43) | copy-start | bytes 1572868
  116.0 3.1 %collective-permute-start.5 = (bf16[8,1024]{1,0:T(8,128)(2,1)S(1)}, bf16[8,1024]{1,0:T(8,128)(2,1)S(1)}, u32[]{:S(2)}, u32[]{:S(2)}) collective-permute-start(bf16[8,1024]{1,0:T(8,128)(2,1)S(1)} %slice.73), channel_id=1, source_target_pairs={{4,0},{8,4},{12,8},{16,12},{20,16},{24,20},{28,24},{5,1},{9,5},{13... | collective-permute-start | bytes 49160 | tf_op jit(solution)/shard_map/ppermute | solution.py:19
  122.6 4.3 %copy-start.2 = (bf16[256,1024]{1,0:T(8,128)(2,1)S(1)}, bf16[256,1024]{1,0:T(8,128)(2,1)}, u32[]{:S(2)}) copy-start(bf16[256,1024]{1,0:T(8,128)(2,1)} %copy-done.1) | copy-start | bytes 1572868
  126.9 2.4 copy-start.8
  145.9 45.9 %copy-start.4 = (f32[64,64]{1,0:T(8,128)S(1)}, f32[64,64]{1,0:T(8,128)}, u32[]{:S(2)}) copy-start(f32[64,64]{1,0:T(8,128)} %get-tuple-element.108) | copy-start | bytes 49156
Sparse Core Ops, SparseCore 0:
  30.4 81.6 all-gather.10
  114.0 70.4 all-gather.6
  186.4 39.7 all-gather.8
  230.4 27.2 reduce-scatter.1
